TPU v7x, 128 devices: a whole 4x4x4 slice. The times are simulated.
128 devices in a mesh: ctx: 32 (over y, z, core), exp: 4 (over x).
Axes of the slice: x: 4, y: 4, z: 4, core: 2. Of those that a mesh axis runs over, the one named last changes fastest.
Arguments:
- inputs: bfloat16 [4096, 4096], P('ctx', 'exp'), may hold values from -6 to 6
- gate_input: bfloat16 [4096, 4096], P('ctx', 'exp')
- b_proj: bfloat16 [4096, 128], P('ctx'), may hold values from -0.5 to 0.5
- c_proj: bfloat16 [4096, 128], P('ctx'), may hold values from -6 to 6
- step_size: float32 [64, 4096], P('exp', 'ctx'), may hold values from 0.03 to 0.3
- decay_rate: float32 [64, 4096], P('exp', 'ctx'), as said below
- skip_gain: float32 [64], P('exp'), may hold values from 0.5 to 2
- start_state: float32 [64, 64, 128], P('exp'), may hold values from -3 to 3
- norm_gain: float32 [4096], P('exp'), may hold values from 0.5 to 1.5
- out_proj: bfloat16 [4096, 4096], P('exp', 'ctx'), may hold values from -0.09375 to 0.09375
- residual: bfloat16 [4096, 4096], P('ctx'), may hold values from -6 to 6
- moe_gain: float32 [4096], replicated, may hold values from 0.5 to 1.5
- w_gate: bfloat16 [32, 4096, 3584], P('ctx', None, 'exp'), may hold values from -0.09375 to 0.09375
- w_up: bfloat16 [32, 4096, 3584], P('ctx', None, 'exp'), may hold values from -0.09375 to 0.09375
- w_down: bfloat16 [32, 3584, 4096], P('ctx', 'exp'), may hold values from -0.0625 to 0.0625
- route_ids: int32 [4096, 2], P('ctx'), may hold values from 0 to 15, all different within a row; in each aligned block of 32 rows (0 to 31, 32 to 63, ...) at most 8 rows name the same one
- route_gates: float32 [4096, 2], P('ctx'), may hold values from 0.3 to 1
Outputs:
- output: bfloat16 [4096, 4096], P(('ctx', 'exp'))
Inputs may be any that keep to these rules, and one draw needn't show every extreme that they name: `route_ids`: each row names two different experts. In each aligned block of 32 rows no expert is named more than 8 times, a bound that some block reaches. `decay_rate`: Non-negative.
All inputs are finite; a program needn't handle non-finite values.
Results may differ from a plain program's by a relative error of at most 0.02.
Values may be sent and summed in bfloat16 or wider, within the bound.
A program may use at most 128 MiB of HBM per device.

v0:
```python
import jax
import jax.numpy as jnp
from jax import lax
from jax.sharding import PartitionSpec as P

PAIR = 2
eps_norm = 1e-05
top_precision = lax.Precision.HIGHEST


def entering(x, axis, join, neutral):
    place = lax.axis_index(axis)
    gathered = jax.tree.map(
        lambda a, kind: lax.all_gather(a.astype(kind), axis), x, (jnp.bfloat16, jnp.bfloat16)
    )
    state = jax.tree.map(lambda a, e: jnp.zeros_like(a) + jnp.asarray(e, a.dtype), x, neutral)

    def one(hop, state):
        return join(
            state,
            jax.tree.map(
                lambda a, own: lax.dynamic_index_in_dim(a, hop, 0, False).astype(own.dtype),
                gathered,
                x,
            ),
        )

    return lax.fori_loop(0, place, one, state)


def later_state(earlier, later):
    first_decay, first_state = earlier
    second_decay, second_state = later
    return (first_decay * second_decay, second_decay[:, None, None] * first_state + second_state)


def route_ranks(quarter_ids, experts):
    flattened = quarter_ids.reshape(-1)
    onehot = (flattened[:, None] == jnp.arange(experts, dtype=jnp.int32)[None, :]).astype(jnp.int32)
    running = jnp.cumsum(onehot, axis=0)
    rank_ids = jnp.sum(onehot * running, axis=1) - 1
    return (flattened, rank_ids)


def place_rows(normed, quarter_ids, experts, capacity):
    flattened, rank_ids = route_ranks(quarter_ids, experts)
    slot_ids = rank_ids * experts + flattened
    matches = (
        jnp.arange(capacity * experts, dtype=jnp.int32)[:, None] == slot_ids[None, :]
    ).astype(jnp.bfloat16)
    doubled = jnp.repeat(normed, quarter_ids.shape[1], axis=0)
    placed = jnp.dot(matches, doubled, preferred_element_type=jnp.float32).astype(jnp.bfloat16)
    return placed.reshape(capacity, experts, normed.shape[1])


def rms_rows(values, gain_vec):
    scaling = lax.rsqrt(jnp.mean(values * values, axis=1, keepdims=True) + eps_norm)
    return (values * scaling * gain_vec[None, :]).astype(jnp.bfloat16)


def local(
    inputs,
    gate_input,
    b_proj,
    c_proj,
    step_size,
    decay_rate,
    skip_gain,
    start_state,
    norm_gain,
    out_proj,
    residual,
    moe_gain,
    w_gate,
    w_up,
    w_down,
    route_ids,
    route_gates,
):
    tok_ctx = inputs.shape[0]
    head_count = step_size.shape[0]
    head_dim = inputs.shape[1] // head_count
    model_width = residual.shape[1]
    n_ctx = lax.axis_size("ctx")
    n_exp = lax.axis_size("exp")
    experts = n_ctx // PAIR
    tok_quarter = tok_ctx // n_exp
    capacity = 4 * tok_quarter // experts
    x_local = inputs.astype(jnp.float32).reshape(tok_ctx, head_count, head_dim)
    b_local = b_proj.astype(jnp.float32)
    c_local = c_proj.astype(jnp.float32)
    cumulative = jnp.cumsum(decay_rate, axis=1)
    span_total = cumulative[:, -1]
    sequence_indices = jnp.arange(tok_ctx, dtype=jnp.int32)
    causal = sequence_indices[:, None] >= sequence_indices[None, :]
    spread = jnp.where(causal[None], cumulative[:, :, None] - cumulative[:, None, :], 0.0)
    scores = jnp.dot(c_local, b_local.T, precision=top_precision)
    mixing = jnp.where(causal[None], jnp.exp(-spread), 0.0) * scores[None] * step_size[:, None, :]
    inside_part = jnp.einsum("hts,shp->thp", mixing, x_local, precision=top_precision)
    ending = jnp.exp(-(span_total[:, None] - cumulative)) * step_size
    local_state = jnp.einsum("hs,shp,sn->hpn", ending, x_local, b_local, precision=top_precision)
    prior_decay, prior_state = entering(
        (jnp.exp(-span_total), local_state),
        "ctx",
        later_state,
        (jnp.ones_like(span_total), jnp.zeros_like(local_state)),
    )
    incoming = prior_state + prior_decay[:, None, None] * start_state
    carried = (
        jnp.einsum("hpn,tn->thp", incoming, c_local, precision=top_precision)
        * jnp.exp(-cumulative).T[:, :, None]
    )
    ssm_out = inside_part + carried + skip_gain[None, :, None] * x_local
    gated_out = ssm_out.reshape(tok_ctx, head_count * head_dim) * jax.nn.silu(
        gate_input.astype(jnp.float32)
    )
    squares = lax.psum(jnp.sum(gated_out * gated_out, axis=1), "exp")
    scaling = lax.rsqrt(squares / (head_count * head_dim * n_exp) + eps_norm)
    normed_mix = (gated_out * scaling[:, None] * norm_gain[None, :]).astype(jnp.bfloat16)
    partial_value = jnp.dot(
        normed_mix,
        lax.all_gather(out_proj, "ctx", axis=1, tiled=True),
        preferred_element_type=jnp.float32,
    )
    gate_rows = w_gate[0]
    up_rows = w_up[0]
    down_rows = w_down[0]
    piece_width = gate_rows.shape[1]
    first_row = lax.axis_index("exp") * tok_quarter
    own_ids = lax.dynamic_slice_in_dim(route_ids, first_row, tok_quarter, 0)
    own_gates = lax.dynamic_slice_in_dim(route_gates, first_row, tok_quarter, 0)
    mixed_all = lax.psum(partial_value.astype(jnp.bfloat16), "exp").astype(jnp.float32)
    hidden_all = residual.astype(jnp.float32) + mixed_all
    moe_all = rms_rows(hidden_all, moe_gain)

    def place_quarter(quarter_rows, quarter_ids):
        return place_rows(quarter_rows, quarter_ids, experts, capacity)

    placed = jax.vmap(place_quarter)(
        moe_all.reshape(n_exp, tok_quarter, model_width),
        route_ids.reshape(n_exp, tok_quarter, route_ids.shape[1]),
    )
    placed = placed.reshape(n_exp * capacity, experts, model_width)
    outgoing = jnp.repeat(placed, PAIR, axis=1)
    arrived = lax.all_to_all(outgoing, "ctx", split_axis=1, concat_axis=1, tiled=True)
    flattened = arrived.reshape(-1, model_width)
    gate_val = jnp.dot(flattened, gate_rows, preferred_element_type=jnp.float32)
    up_val = jnp.dot(flattened, up_rows, preferred_element_type=jnp.float32)
    activated = (jax.nn.silu(gate_val) * up_val).astype(jnp.bfloat16)
    hidden = activated.reshape(arrived.shape[0], arrived.shape[1], piece_width)
    hidden_own = lax.dynamic_slice_in_dim(hidden_all, first_row, tok_quarter, 0)
    product = jnp.dot(
        hidden.reshape(-1, piece_width), down_rows, preferred_element_type=jnp.float32
    )
    rounded = lax.optimization_barrier(product.astype(jnp.bfloat16)).astype(jnp.float32)
    summed = lax.psum_scatter(
        rounded.reshape(lax.axis_size("exp") * capacity, hidden.shape[1], model_width).astype(
            jnp.bfloat16
        ),
        "exp",
        scatter_dimension=0,
        tiled=True,
    )
    halves = lax.all_to_all(summed, "ctx", split_axis=1, concat_axis=1, tiled=True)
    flattened, rank_ids = route_ranks(own_ids, experts)
    base_rows = rank_ids * n_ctx + flattened * PAIR
    fetch_rows = base_rows[:, None] + jnp.arange(PAIR, dtype=jnp.int32)[None, :]
    fetched = halves.reshape(capacity * n_ctx, model_width)[fetch_rows]
    expert_out = jnp.sum(fetched.astype(jnp.float32), axis=1)
    weighted = expert_out * own_gates.reshape(-1)[:, None]
    moe_out = jnp.sum(weighted.reshape(tok_quarter, -1, model_width), axis=1)
    return (hidden_own + moe_out).astype(jnp.bfloat16)


def solution(mesh):
    in_specs = (
        P("ctx", "exp"),
        P("ctx", "exp"),
        P("ctx", None),
        P("ctx", None),
        P("exp", "ctx"),
        P("exp", "ctx"),
        P("exp"),
        P("exp", None, None),
        P("exp"),
        P("exp", "ctx"),
        P("ctx", None),
        P(),
        P("ctx", None, "exp"),
        P("ctx", None, "exp"),
        P("ctx", "exp", None),
        P("ctx", None),
        P("ctx", None),
    )
    out_specs = P(("ctx", "exp"), None)
    return jax.shard_map(local, mesh=mesh, in_specs=in_specs, out_specs=out_specs, check_vma=False)
```

profile of v0, /device:TPU:1, one launch (start us, length us, event | category | flops | bytes accessed | tf_op | source)
XLA Modules:
  0.0 490.3 jit_solution(6920894452097007620)
XLA Ops:
  6.5 1.0 reduce_window_sum.33
  7.5 0.2 slice_reduce_fusion
  7.7 1.1 copy.61
  8.8 0.8 exponential_bitcast_fusion
  9.6 1.1 convolution_convert_fusion.3
  10.8 0.7 all-gather.5.cloned.1.call-update
  11.6 1.2 dynamic-slice
  13.4 0.2 fusion.38
  13.6 0.2 dynamic-update-slice
  13.8 65.5 %all-reduce = bf16[512]{0:T(512)(128)(2,1)S(1)} all-reduce(bf16[512]{0:T(512)(128)(2,1)S(1)} %dynamic-update-slice), channel_id=2, replica_groups=mesh['ctx'=32,'exp'=4] {'ctx'}, use_global_device_ids=true, to_apply=%add | all-reduce | flops 512 | bytes 2048
  79.5 0.9 fusion.42
  80.5 1.2 while.12
  80.5 1.1 convert_add_fusion.3
  81.7 0.5 fusion.9
  82.2 1.4 fusion.8
  83.6 0.2 copy.62
  83.8 0.2 multiply_reduce_fusion.2
  84.1 8.4 %psum.14 = f32[128]{0:T(128)S(1)} all-reduce(f32[128]{0:T(128)S(1)} %multiply_reduce_fusion.2), channel_id=1, replica_groups=mesh['ctx'=32,'exp'=4] {'exp'}, use_global_device_ids=true, to_apply=%region_4.5 | all-reduce | flops 128 | bytes 1024 | tf_op jit(solution)/shard_map/psum | solution.py:117
  92.5 36.7 %all-gather.5.cloned.1.call-done = bf16[1024,4096]{1,0:T(8,128)(2,1)} async-done(((bf16[1024,128]{1,0:T(8,128)(2,1)}), bf16[1024,4096]{1,0:T(8,128)(2,1)}) %all-gather.5.cloned.1.call-update) | async-done | bytes 8388624 | tf_op jit(solution)/shard_map/all_gather | solution.py:122
  129.2 5.8 %convolution_convert_fusion.2 = bf16[128,4096]{1,0:T(8,128)(2,1)} fusion(bf16[1024,4096]{1,0:T(8,128)(2,1)} %all-gather.5.cloned.1.call-done, f32[1024]{0:T(1024)S(1)} %copy-done.12, f32[128]{0:T(128)S(1)} %add_rsqrt_fusion.1, f32[128,1024]{1,0:T(8,128)S(1)} %copy.62, bf16[128,1024]{1,0:T(8,128)(2,1)S(1)} %copy-done.6), kind=kOutput, calls=%fused_computation.10 | convolution fusion | flops 1075445760 | bytes 10228224 | tf_op jit(solution)/shard_map/dot_general | solution.py:120
  135.5 0.1 reduce_window_sum.34
  135.6 0.2 select_reduce_fusion
  135.8 42.9 %all-reduce.3.cloned.1.call-done = bf16[128,4096]{1,0:T(8,128)(2,1)} async-done(((bf16[128,4096]{1,0:T(8,128)(2,1)}), bf16[128,4096]{1,0:T(8,128)(2,1)}) %all-reduce.3.cloned.1.call-update) | async-done | bytes 1048592 | tf_op jit(solution)/shard_map/psum | solution.py:132
  178.8 3.0 convert_add_fusion.1
  181.8 0.4 multiply_convert_fusion.1
  182.2 3.4 broadcast_in_dim.28
  185.7 2.7 reshape.157
  188.4 1.4 convolution_convert_fusion.1
  189.8 2.3 copy.64
  192.1 4.3 broadcast_in_dim.29
  196.3 105.0 %all_to_all.10 = bf16[32,32,4096]{2,0,1:T(8,128)(2,1)} all-to-all(bf16[32,32,4096]{2,0,1:T(8,128)(2,1)} %bitcast.66), channel_id=1, replica_groups=mesh['ctx'=32,'exp'=4] {'ctx'}, dimensions={1} | all-to-all | bytes 16777216 | tf_op jit(solution)/shard_map/all_to_all | solution.py:145
  301.4 11.3 %copy.65 = bf16[32,32,4096]{2,1,0:T(8,128)(2,1)} copy(bf16[32,32,4096]{2,0,1:T(8,128)(2,1)} %all_to_all.10) | data formatting | bytes 16777216 | tf_op jit(solution)/shard_map/all_to_all | solution.py:145
  312.7 13.0 %fusion.1 = f32[1024,896]{1,0:T(8,128)S(1)} fusion(bf16[1024,4096]{1,0:T(8,128)(2,1)} %bitcast.68, bf16[1,4096,896]{2,1,0:T(8,128)(2,1)} %param.32), kind=kOutput, calls=%fused_computation.5 | convolution fusion | flops 7516192768 | bytes 19398656 | tf_op jit(solution)/shard_map/dot_general | solution.py:148
  325.8 9.2 %multiply_convert_fusion = bf16[1024,896]{1,0:T(8,128)(2,1)S(1)} fusion(f32[1024,896]{1,0:T(8,128)S(1)} %fusion.1, bf16[1024,4096]{1,0:T(8,128)(2,1)S(1)} %bitcast.69, bf16[1,4096,896]{2,1,0:T(8,128)(2,1)S(1)} %bitcast.78), kind=kOutput, calls=%fused_computation.11 | convolution fusion | flops 7521697792 | bytes 21233664 | tf_op jit(solution)/shard_map/dot_general | solution.py:147
  335.0 11.2 %convolution_convert_fusion = bf16[1024,4096]{1,0:T(8,128)(2,1)} fusion(bf16[1024,896]{1,0:T(8,128)(2,1)S(1)} %multiply_convert_fusion, bf16[1,896,4096]{2,1,0:T(8,128)(2,1)S(1)} %bitcast.80), kind=kOutput, calls=%fused_computation.3 | convolution fusion | flops 7520387072 | bytes 17563648 | tf_op jit(solution)/shard_map/dot_general | solution.py:152
  346.2 11.3 %copy.74 = bf16[4,8,32,4096]{3,1,2,0:T(8,128)(2,1)} copy(bf16[4,8,32,4096]{3,2,1,0:T(8,128)(2,1)} %bitcast.70) | data formatting | bytes 16777216
  357.5 77.8 %reduce-scatter.4.cloned.1.call-done = bf16[8,131072]{1,0:T(8,128)(2,1)} async-done(((bf16[32,131072]{1,0:T(8,128)(2,1)}), bf16[8,131072]{1,0:T(8,128)(2,1)}) %reduce-scatter.4.cloned.1.call-update) | async-done | bytes 2097168
  435.3 8.1 %all-to-all-start.1 = ((bf16[8,32,4096]{2,0,1:T(8,128)(2,1)}), bf16[8,32,4096]{2,0,1:T(8,128)(2,1)}, u32[]{:S(2)}, u32[]{:S(2)}) async-start(bf16[8,32,4096]{2,0,1:T(8,128)(2,1)} %bitcast.72), calls=%async_computation.1 | async-start | bytes 4194304 | tf_op jit(solution)/shard_map/all_to_all | solution.py:164
  443.9 0.2 select_reduce_fusion.1
  444.2 0.1 reshape.166
  444.5 27.1 %all-to-all-done.1 = bf16[8,32,4096]{2,0,1:T(8,128)(2,1)} async-done(((bf16[8,32,4096]{2,0,1:T(8,128)(2,1)}), bf16[8,32,4096]{2,0,1:T(8,128)(2,1)}, u32[]{:S(2)}, u32[]{:S(2)}) %all-to-all-start.1) | async-done | bytes 2097184 | tf_op jit(solution)/shard_map/all_to_all | solution.py:164
  471.6 2.7 copy.67
  474.3 1.2 gather_fusion
  475.5 1.3 reshape.175
  476.9 2.7 reduce_sum.60
  479.6 0.6 reduce_sum.61
  480.2 1.4 multiply_reduce_fusion.1
  481.7 1.8 add_convert_fusion
  (68 shorter events, 1.5 us)
Async XLA Ops:
  6.5 3.1 copy-start
  6.5 73.9 %all-gather.7.cloned.1.call-start = ((), (), s32[]{:S(2)}) async-start(), calls=%async_computation.5 | async-start | bytes 8650752 | tf_op jit(solution)/shard_map/all_gather | solution.py:14
  10.7 118.4 %all-gather.5.cloned.1.call-start = ((), (), s32[]{:S(2)}) async-start(), calls=%async_computation.3 | async-start | bytes 8650752 | tf_op jit(solution)/shard_map/all_gather | solution.py:122
  11.5 167.3 %all-reduce.3.cloned.1.call-start = ((), (), s32[]{:S(2)}) async-start(), calls=%async_computation.4 | async-start | bytes 2097152 | tf_op jit(solution)/shard_map/psum | solution.py:132
  80.3 1.4 copy-start.5
  80.3 1.4 copy-start.7
  80.5 1.7 copy-start.9
  80.5 1.7 copy-start.13
  81.7 2.1 copy-start.6
  81.7 47.5 %copy-start.12 = (f32[1024]{0:T(1024)S(1)}, f32[1024]{0:T(1024)}, u32[]{:S(2)}) copy-start(f32[1024]{0:T(1024)} %param.27) | copy-start | bytes 12292
  92.5 42.6 %copy-start.10 = (s32[128,2]{0,1:T(2,128)S(1)}, s32[128,2]{0,1:T(2,128)}, u32[]{:S(2)}) copy-start(s32[128,2]{0,1:T(2,128)} %param.34) | copy-start | bytes 3076
  92.5 86.3 %copy-start.3 = (bf16[128,4096]{1,0:T(8,128)(2,1)S(1)}, bf16[128,4096]{1,0:T(8,128)(2,1)}, u32[]{:S(2)}) copy-start(bf16[128,4096]{1,0:T(8,128)(2,1)} %param.29) | copy-start | bytes 3145732
  135.0 46.8 %copy-start.8 = (f32[4096]{0:T(1024)S(1)}, f32[4096]{0:T(1024)}, u32[]{:S(2)}) copy-start(f32[4096]{0:T(1024)} %param.30) | copy-start | bytes 49156
  135.1 300.3 %reduce-scatter.4.cloned.1.call-start = ((), (), s32[]{:S(2)}) async-start(), calls=%async_computation.6 | async-start | bytes 10485760
  178.8 3.0 copy-start.4
  301.4 24.4 %slice-start = ((s8[7340032]{0:T(1024)(128)(4,1)}), s8[3145728]{0:T(1024)(128)(4,1)S(1)}, s32[]{:S(2)}) async-start(s8[7340032]{0:T(1024)(128)(4,1)} %bitcast.77), calls=%async_computation.7 | async-start | bytes 6291456
  312.7 13.0 %copy-start.2 = (bf16[32,32,4096]{2,1,0:T(8,128)(2,1)S(1)}, bf16[32,32,4096]{2,1,0:T(8,128)(2,1)}, u32[]{:S(2)}) copy-start(bf16[32,32,4096]{2,1,0:T(8,128)(2,1)} %copy.65) | copy-start | bytes 25165828
  312.7 13.0 %slice-start.1 = ((s8[7340032]{0:T(1024)(128)(4,1)}), s8[4194304]{0:T(1024)(128)(4,1)S(1)}, s32[]{:S(2)}) async-start(s8[7340032]{0:T(1024)(128)(4,1)} %bitcast.77), calls=%async_computation.8 | async-start | bytes 8388608
  312.7 22.2 %slice-start.2 = ((s8[7340032]{0:T(1024)(128)(4,1)}), s8[4194304]{0:T(1024)(128)(4,1)S(1)}, s32[]{:S(2)}) async-start(s8[7340032]{0:T(1024)(128)(4,1)} %bitcast.79), calls=%async_computation.9 | async-start | bytes 8388608
  325.8 9.2 %slice-start.3 = ((s8[7340032]{0:T(1024)(128)(4,1)}), s8[3145728]{0:T(1024)(128)(4,1)S(1)}, s32[]{:S(2)}) async-start(s8[7340032]{0:T(1024)(128)(4,1)} %bitcast.79), calls=%async_computation.10 | async-start | bytes 6291456
  357.5 86.8 %copy-start.11 = (f32[128,2]{0,1:T(2,128)S(1)}, f32[128,2]{0,1:T(2,128)}, u32[]{:S(2)}) copy-start(f32[128,2]{0,1:T(2,128)} %param.35) | copy-start | bytes 3076
  435.3 36.3 %all-to-all-start.1 = ((bf16[8,32,4096]{2,0,1:T(8,128)(2,1)}), bf16[8,32,4096]{2,0,1:T(8,128)(2,1)}, u32[]{:S(2)}, u32[]{:S(2)}) async-start(bf16[8,32,4096]{2,0,1:T(8,128)(2,1)} %bitcast.72), calls=%async_computation.1 | async-start | bytes 4194304 | tf_op jit(solution)/shard_map/all_to_all | solution.py:164
  475.5 8.0 %copy-start.1 = (bf16[128,128]{1,0:T(8,128)(2,1)S(1)}, bf16[128,128]{1,0:T(8,128)(2,1)}, u32[]{:S(2)}) copy-start(bf16[128,128]{1,0:T(8,128)(2,1)} %param.21) | copy-start | bytes 98308
Sparse Core Ops, SparseCore 0:
  10.9 56.8 all-gather.6
  69.9 59.2 all-gather.4
  135.2 43.5 all-reduce.2
  357.7 77.6 reduce-scatter.3
where the time goes:
time: 500 us; the launch traced here: 490 us
  waiting for transfers between devices  185 us (37%)
  blocking collectives  179 us (36%)
  local copies, waits for them, and re-layouts  45.3 us (9%)
  matrix products  44.4 us (9%)
  between operations  14.4 us (3%)
  other arithmetic  13.7 us (3%)
  starting transfers between devices  8.24 us (2%)
    all_to_all x1, blocking collectives, local(): lax.all_to_all(outgoing, 'ctx', split_axis=1, concat_axis=1, tiled=True)  105 us
    unnamed x5, waiting for transfers between devices  78.5 us
    unnamed x1, blocking collectives  65.5 us
    psum x1, waiting for transfers between devices, local(): lax.psum(partial_value.astype(jnp.bfloat16), 'exp').astype(jnp.float32)  42.9 us
    all_gather x1, waiting for transfers between devices, local(): lax.all_gather(out_proj, 'ctx', axis=1, tiled=True)  36.7 us
    all_to_all x1, waiting for transfers between devices, local(): lax.all_to_all(summed, 'ctx', split_axis=1, concat_axis=1, tiled=True)  27.1 us
    unnamed x42, local copies, waits for them, and re-layouts  14.1 us
    dot_general x1, matrix products, local(): up_val = jnp.dot(flattened, up_rows, preferred_element_type=jnp.float32)  13 us
  transfers between devices with their start and end apart: 5, of which 4 were waited for; matrix products, arithmetic and copies ran while one was open for 2% of the time, Pallas kernels for 0%

commit v1 on v0

--- a/solution.py
+++ b/solution.py
@@ -129,7 +129,9 @@
     first_row = lax.axis_index("exp") * tok_quarter
     own_ids = lax.dynamic_slice_in_dim(route_ids, first_row, tok_quarter, 0)
     own_gates = lax.dynamic_slice_in_dim(route_gates, first_row, tok_quarter, 0)
-    mixed_all = lax.psum(partial_value.astype(jnp.bfloat16), "exp").astype(jnp.float32)
+    mixed_all = jnp.sum(lax.all_gather(partial_value.astype(jnp.bfloat16), "exp"), axis=0).astype(
+        jnp.float32
+    )
     hidden_all = residual.astype(jnp.float32) + mixed_all
     moe_all = rms_rows(hidden_all, moe_gain)
 

time: 500 us -> 500 us (level)
    all_gather x0 -> x1, waiting for transfers between devices: none -> 46.5 us  [local(): lax.all_gather(partial_value.astype(jnp.bfloat16), 'exp')]
    psum x1 -> x0, waiting for transfers between devices: 42.9 us -> none  [local(): lax.psum(partial_value.astype(jnp.bfloat16), 'exp').astype(jnp.float32)]
    unnamed x42 -> x40, local copies, waits for them, and re-layouts: 14.1 us -> 14.1 us
where the time goes in v1:
time: 500 us; the launch traced here: 494 us
  waiting for transfers between devices  188 us (38%)
  blocking collectives  178 us (36%)
  local copies, waits for them, and re-layouts  45.3 us (9%)
  matrix products  44.1 us (9%)
  other arithmetic  15.5 us (3%)
  between operations  14.4 us (3%)
  starting transfers between devices  8.55 us (2%)
    all_to_all x1, blocking collectives, local(): lax.all_to_all(outgoing, 'ctx', split_axis=1, concat_axis=1, tiled=True)  104 us
    unnamed x5, waiting for transfers between devices  78 us
    unnamed x1, blocking collectives  65.5 us
    all_gather x1, waiting for transfers between devices, local(): lax.all_gather(partial_value.astype(jnp.bfloat16), 'exp')  46.5 us
    all_gather x1, waiting for transfers between devices, local(): lax.all_gather(out_proj, 'ctx', axis=1, tiled=True)  36.7 us
    all_to_all x1, waiting for transfers between devices, local(): lax.all_to_all(summed, 'ctx', split_axis=1, concat_axis=1, tiled=True)  27.1 us
    unnamed x40, local copies, waits for them, and re-layouts  14.1 us
    dot_general x1, matrix products, local(): up_val = jnp.dot(flattened, up_rows, preferred_element_type=jnp.float32)  12.7 us
  transfers between devices with their start and end apart: 5, of which 4 were waited for; matrix products, arithmetic and copies ran while one was open for 2% of the time, Pallas kernels for 0%

profile of v1, /device:TPU:1, one launch (start us, length us, event | category | flops | bytes accessed | tf_op | source)
XLA Modules:
  0.0 494.0 jit_solution(18223204004579888819)
XLA Ops:
  6.5 1.0 reduce_window_sum.33
  7.5 0.2 slice_reduce_fusion
  7.7 1.1 copy.61
  8.8 0.8 exponential_bitcast_fusion
  9.6 1.1 convolution_convert_fusion.3
  10.8 0.7 all-gather.7.cloned.1.call-update
  11.6 1.2 dynamic-slice
  13.4 0.2 fusion.38
  13.6 0.2 dynamic-update-slice
  13.8 65.5 %all-reduce = bf16[512]{0:T(512)(128)(2,1)S(1)} all-reduce(bf16[512]{0:T(512)(128)(2,1)S(1)} %dynamic-update-slice), channel_id=2, replica_groups=mesh['ctx'=32,'exp'=4] {'ctx'}, use_global_device_ids=true, to_apply=%add | all-reduce | flops 512 | bytes 2048
  79.5 0.9 fusion.42
  80.5 1.2 while.12
  80.5 1.1 convert_add_fusion.3
  81.7 0.5 fusion.9
  82.2 1.4 fusion.8
  83.6 0.2 copy.62
  83.8 0.2 multiply_reduce_fusion.2
  84.1 8.4 %psum.7 = f32[128]{0:T(128)S(1)} all-reduce(f32[128]{0:T(128)S(1)} %multiply_reduce_fusion.2), channel_id=1, replica_groups=mesh['ctx'=32,'exp'=4] {'exp'}, use_global_device_ids=true, to_apply=%region_4.5 | all-reduce | flops 128 | bytes 1024 | tf_op jit(solution)/shard_map/psum | solution.py:117
  92.5 36.7 %all-gather.7.cloned.1.call-done = bf16[1024,4096]{1,0:T(8,128)(2,1)} async-done(((bf16[1024,128]{1,0:T(8,128)(2,1)}), bf16[1024,4096]{1,0:T(8,128)(2,1)}) %all-gather.7.cloned.1.call-update) | async-done | bytes 8388624 | tf_op jit(solution)/shard_map/all_gather | solution.py:122
  129.2 5.8 %convolution_convert_fusion.2 = bf16[128,4096]{1,0:T(8,128)(2,1)} fusion(bf16[1024,4096]{1,0:T(8,128)(2,1)} %all-gather.7.cloned.1.call-done, f32[1024]{0:T(1024)S(1)} %copy-done.11, f32[128]{0:T(128)S(1)} %add_rsqrt_fusion.1, f32[128,1024]{1,0:T(8,128)S(1)} %copy.62, bf16[128,1024]{1,0:T(8,128)(2,1)S(1)} %copy-done.5), kind=kOutput, calls=%fused_computation.10 | convolution fusion | flops 1075445760 | bytes 10228224 | tf_op jit(solution)/shard_map/dot_general | solution.py:120
  135.1 0.3 reduce-scatter.4.cloned.1.call-start
  135.9 0.2 select_reduce_fusion
  136.1 46.5 %all-gather.11.cloned.1.call-done = bf16[512,4096]{1,0:T(8,128)(2,1)} async-done(((bf16[128,4096]{1,0:T(8,128)(2,1)}), bf16[512,4096]{1,0:T(8,128)(2,1)}) %all-gather.11.cloned.1.call-update) | async-done | bytes 4194320 | tf_op jit(solution)/shard_map/all_gather | solution.py:132
  182.6 3.1 reduce_sum.69
  185.7 1.7 convert_add_fusion.1
  187.4 0.4 multiply_convert_fusion.1
  187.8 3.4 broadcast_in_dim.28
  191.3 2.7 reshape.157
  194.0 1.4 convolution_convert_fusion.1
  195.4 2.3 copy.64
  197.7 4.3 broadcast_in_dim.29
  202.0 103.9 %all_to_all.10 = bf16[32,32,4096]{2,0,1:T(8,128)(2,1)} all-to-all(bf16[32,32,4096]{2,0,1:T(8,128)(2,1)} %bitcast.67), channel_id=1, replica_groups=mesh['ctx'=32,'exp'=4] {'ctx'}, dimensions={1} | all-to-all | bytes 16777216 | tf_op jit(solution)/shard_map/all_to_all | solution.py:147
  305.9 11.3 %copy.65 = bf16[32,32,4096]{2,1,0:T(8,128)(2,1)} copy(bf16[32,32,4096]{2,0,1:T(8,128)(2,1)} %all_to_all.10) | data formatting | bytes 16777216 | tf_op jit(solution)/shard_map/all_to_all | solution.py:147
  317.2 12.7 %fusion.1 = f32[1024,896]{1,0:T(8,128)S(1)} fusion(bf16[1024,4096]{1,0:T(8,128)(2,1)} %bitcast.69, bf16[1,4096,896]{2,1,0:T(8,128)(2,1)} %param.32), kind=kOutput, calls=%fused_computation.5 | convolution fusion | flops 7516192768 | bytes 19398656 | tf_op jit(solution)/shard_map/dot_general | solution.py:150
  329.9 9.2 %multiply_convert_fusion = bf16[1024,896]{1,0:T(8,128)(2,1)S(1)} fusion(f32[1024,896]{1,0:T(8,128)S(1)} %fusion.1, bf16[1024,4096]{1,0:T(8,128)(2,1)S(1)} %bitcast.70, bf16[1,4096,896]{2,1,0:T(8,128)(2,1)S(1)} %bitcast.80), kind=kOutput, calls=%fused_computation.11 | convolution fusion | flops 7521697792 | bytes 21233664 | tf_op jit(solution)/shard_map/dot_general | solution.py:149
  339.1 11.3 %convolution_convert_fusion = bf16[1024,4096]{1,0:T(8,128)(2,1)} fusion(bf16[1024,896]{1,0:T(8,128)(2,1)S(1)} %multiply_convert_fusion, bf16[1,896,4096]{2,1,0:T(8,128)(2,1)S(1)} %bitcast.82), kind=kOutput, calls=%fused_computation.3 | convolution fusion | flops 7520387072 | bytes 17563648 | tf_op jit(solution)/shard_map/dot_general | solution.py:154
  350.4 11.3 %copy.74 = bf16[4,8,32,4096]{3,1,2,0:T(8,128)(2,1)} copy(bf16[4,8,32,4096]{3,2,1,0:T(8,128)(2,1)} %bitcast.71) | data formatting | bytes 16777216
  361.7 77.2 %reduce-scatter.4.cloned.1.call-done = bf16[8,131072]{1,0:T(8,128)(2,1)} async-done(((bf16[32,131072]{1,0:T(8,128)(2,1)}), bf16[8,131072]{1,0:T(8,128)(2,1)}) %reduce-scatter.4.cloned.1.call-update) | async-done | bytes 2097168
  439.0 8.1 %all-to-all-start.1 = ((bf16[8,32,4096]{2,0,1:T(8,128)(2,1)}), bf16[8,32,4096]{2,0,1:T(8,128)(2,1)}, u32[]{:S(2)}, u32[]{:S(2)}) async-start(bf16[8,32,4096]{2,0,1:T(8,128)(2,1)} %bitcast.74), calls=%async_computation.1 | async-start | bytes 4194304 | tf_op jit(solution)/shard_map/all_to_all | solution.py:166
  447.6 0.2 select_reduce_fusion.1
  448.2 27.1 %all-to-all-done.1 = bf16[8,32,4096]{2,0,1:T(8,128)(2,1)} async-done(((bf16[8,32,4096]{2,0,1:T(8,128)(2,1)}), bf16[8,32,4096]{2,0,1:T(8,128)(2,1)}, u32[]{:S(2)}, u32[]{:S(2)}) %all-to-all-start.1) | async-done | bytes 2097184 | tf_op jit(solution)/shard_map/all_to_all | solution.py:166
  475.3 2.7 copy.67
  478.0 1.2 gather_fusion
  479.2 1.3 reshape.176
  480.6 2.7 reduce_sum.73
  483.3 0.6 reduce_sum.74
  483.9 1.4 multiply_reduce_fusion.1
  485.3 1.8 add_convert_fusion
  (67 shorter events, 1.8 us)
Async XLA Ops:
  6.5 3.1 copy-start
  6.5 73.9 %all-gather.9.cloned.1.call-start = ((), (), s32[]{:S(2)}) async-start(), calls=%async_computation.4 | async-start | bytes 8650752 | tf_op jit(solution)/shard_map/all_gather | solution.py:14
  10.7 118.4 %all-gather.7.cloned.1.call-start = ((), (), s32[]{:S(2)}) async-start(), calls=%async_computation.3 | async-start | bytes 8650752 | tf_op jit(solution)/shard_map/all_gather | solution.py:122
  11.5 171.1 %all-gather.11.cloned.1.call-start = ((), (), s32[]{:S(2)}) async-start(), calls=%async_computation.5 | async-start | bytes 5242880 | tf_op jit(solution)/shard_map/all_gather | solution.py:132
  80.3 1.4 copy-start.4
  80.3 1.4 copy-start.6
  80.5 1.7 copy-start.8
  80.5 1.7 copy-start.12
  81.7 2.1 copy-start.5
  81.7 47.5 %copy-start.11 = (f32[1024]{0:T(1024)S(1)}, f32[1024]{0:T(1024)}, u32[]{:S(2)}) copy-start(f32[1024]{0:T(1024)} %param.27) | copy-start | bytes 12292
  92.5 42.9 %copy-start.9 = (s32[128,2]{0,1:T(2,128)S(1)}, s32[128,2]{0,1:T(2,128)}, u32[]{:S(2)}) copy-start(s32[128,2]{0,1:T(2,128)} %param.34) | copy-start | bytes 3076
  135.0 50.7 %copy-start.3 = (bf16[128,4096]{1,0:T(8,128)(2,1)S(1)}, bf16[128,4096]{1,0:T(8,128)(2,1)}, u32[]{:S(2)}) copy-start(bf16[128,4096]{1,0:T(8,128)(2,1)} %param.29) | copy-start | bytes 3145732
  135.1 303.9 %reduce-scatter.4.cloned.1.call-start = ((), (), s32[]{:S(2)}) async-start(), calls=%async_computation.6 | async-start | bytes 10485760
  182.6 4.8 copy-start.7
  305.9 24.0 %slice-start = ((s8[7340032]{0:T(1024)(128)(4,1)}), s8[3145728]{0:T(1024)(128)(4,1)S(1)}, s32[]{:S(2)}) async-start(s8[7340032]{0:T(1024)(128)(4,1)} %bitcast.79), calls=%async_computation.7 | async-start | bytes 6291456
  317.2 12.7 %copy-start.2 = (bf16[32,32,4096]{2,1,0:T(8,128)(2,1)S(1)}, bf16[32,32,4096]{2,1,0:T(8,128)(2,1)}, u32[]{:S(2)}) copy-start(bf16[32,32,4096]{2,1,0:T(8,128)(2,1)} %copy.65) | copy-start | bytes 25165828
  317.2 12.7 %slice-start.1 = ((s8[7340032]{0:T(1024)(128)(4,1)}), s8[4194304]{0:T(1024)(128)(4,1)S(1)}, s32[]{:S(2)}) async-start(s8[7340032]{0:T(1024)(128)(4,1)} %bitcast.79), calls=%async_computation.8 | async-start | bytes 8388608
  317.2 21.9 %slice-start.2 = ((s8[7340032]{0:T(1024)(128)(4,1)}), s8[4194304]{0:T(1024)(128)(4,1)S(1)}, s32[]{:S(2)}) async-start(s8[7340032]{0:T(1024)(128)(4,1)} %bitcast.81), calls=%async_computation.9 | async-start | bytes 8388608
  329.9 9.2 %slice-start.3 = ((s8[7340032]{0:T(1024)(128)(4,1)}), s8[3145728]{0:T(1024)(128)(4,1)S(1)}, s32[]{:S(2)}) async-start(s8[7340032]{0:T(1024)(128)(4,1)} %bitcast.81), calls=%async_computation.10 | async-start | bytes 6291456
  361.7 86.3 %copy-start.10 = (f32[128,2]{0,1:T(2,128)S(1)}, f32[128,2]{0,1:T(2,128)}, u32[]{:S(2)}) copy-start(f32[128,2]{0,1:T(2,128)} %param.35) | copy-start | bytes 3076
  439.0 36.3 %all-to-all-start.1 = ((bf16[8,32,4096]{2,0,1:T(8,128)(2,1)}), bf16[8,32,4096]{2,0,1:T(8,128)(2,1)}, u32[]{:S(2)}, u32[]{:S(2)}) async-start(bf16[8,32,4096]{2,0,1:T(8,128)(2,1)} %bitcast.74), calls=%async_computation.1 | async-start | bytes 4194304 | tf_op jit(solution)/shard_map/all_to_all | solution.py:166
  479.2 8.0 %copy-start.1 = (bf16[128,128]{1,0:T(8,128)(2,1)S(1)}, bf16[128,128]{1,0:T(8,128)(2,1)}, u32[]{:S(2)}) copy-start(bf16[128,128]{1,0:T(8,128)(2,1)} %param.21) | copy-start | bytes 98308
Sparse Core Ops, SparseCore 0:
  10.9 56.8 all-gather.8
  69.9 59.2 all-gather.6
  135.2 47.3 all-gather.10
  361.8 77.0 reduce-scatter.3
